TPU v7x, 32 devices: a whole 2x2x4 slice. The times are simulated.
32 devices in a mesh: order: 4 (over x, core), blk: 8 (over z, y).
Axes of the slice: x: 2, y: 2, z: 4, core: 2. Of those that a mesh axis runs over, the one named last changes fastest.
Arguments:
- emode_coeffs: bfloat16 [4096, 16, 128], P('blk', 'order'), may hold values from -6 to 6
- lensing_coeffs: bfloat16 [4096, 16, 128], P('blk', 'order'), may hold values from -6 to 6
- order_values: int32 [16], replicated, may hold values from 0 to 4095, as said below
- circle_indices: int32 [1024], replicated, may hold values from 0 to 1023, each once
- circle_weights: float32 [1024], replicated, may hold values from 0.25 to 1
Outputs:
- gradient_part: bfloat16 [4096, 16, 128], P('blk', 'order')
- curl_part: bfloat16 [4096, 16, 128], P('blk', 'order')
Inputs may be any that keep to these rules, and one draw needn't show every extreme that they name: `order_values`: distinct; exactly one value lies in each band from b * 256 to (b + 1) * 256 - 1. `circle_indices`: each circle of the sky exactly once.
All inputs are finite; a program needn't handle non-finite values.
Results may differ from a plain program's by a relative error of at most 0.012.
The roundings to bfloat16 on the way count: a program that leaves them out, or rounds other values in their place, can miss the bound.
Values may be sent and summed in bfloat16 or wider, within the bound.
A program may use at most 128 MiB of HBM per device.

v0:
```python
import functools
import math

import jax
import jax.numpy as jnp
from jax import lax
from jax.experimental import pallas as pl
from jax.experimental.pallas import tpu as pltpu
from jax.sharding import PartitionSpec as P

LONGS = 256
BF = jnp.bfloat16
F32 = jnp.float32
MESH = pl.DeviceIdType.MESH


def wrap(value, period):
    if period & (period - 1) == 0:
        return value & (period - 1)
    return jnp.mod(value, period)


def sin_cos(steps, period):
    quarter = period // 4
    steps = wrap(steps, period)
    turn = (steps + quarter // 2) // quarter if quarter & (quarter - 1) else (steps + quarter // 2) >> (quarter.bit_length() - 1)
    x = (steps - turn * quarter).astype(F32) * (2.0 * math.pi / period)
    x2 = x * x
    s = x * (1.0 + x2 * (-1.0 / 6 + x2 * (1.0 / 120 + x2 * (-1.0 / 5040 + x2 * (1.0 / 362880)))))
    c = 1.0 + x2 * (-0.5 + x2 * (1.0 / 24 + x2 * (-1.0 / 720 + x2 * (1.0 / 40320))))
    odd = (turn & 1) == 1
    sine = jnp.where(odd, c, s)
    cosine = jnp.where(odd, s, c)
    sine = jnp.where((turn & 2) == 2, -sine, sine)
    cosine = jnp.where(((turn + 1) & 2) == 2, -cosine, cosine)
    return sine, cosine


def quarter_turns(order):
    turn = order & 3
    c = jnp.where(turn == 0, 1.0, jnp.where(turn == 2, -1.0, 0.0)).astype(F32)
    s = jnp.where(turn == 1, 1.0, jnp.where(turn == 3, -1.0, 0.0)).astype(F32)
    return c, s


def neighbours(order_size, line):
    order_pos, blk = lax.axis_index("order"), lax.axis_index("blk")
    h, y = lax.div(blk, 2), lax.rem(blk, 2)
    pair = blk + 1 - 2 * y
    peers = [lax.rem(order_pos + k, order_size) for k in range(1, order_size)]
    return order_pos, blk, h, y, pair, peers


def greet(order_size, line):
    order_pos, blk, h, y, pair, peers = neighbours(order_size, line)
    barrier = pltpu.get_barrier_semaphore()

    @pl.when(h > 0)
    def _():
        pl.semaphore_signal(barrier, inc=1, device_id={"blk": blk - 2}, device_id_type=MESH)

    @pl.when(h < line - 1)
    def _():
        pl.semaphore_signal(barrier, inc=1, device_id={"blk": blk + 2}, device_id_type=MESH)

    pl.semaphore_signal(barrier, inc=1, device_id={"blk": pair}, device_id_type=MESH)
    for peer in peers:
        pl.semaphore_signal(barrier, inc=1, device_id={"order": peer}, device_id_type=MESH)
    ends = jnp.where(h > 0, 1, 0) + jnp.where(h < line - 1, 1, 0)
    pl.semaphore_wait(barrier, order_size + ends)


def remote(src, dst, send, recv, device):
    return pltpu.make_async_remote_copy(
        src_ref=src, dst_ref=dst, send_sem=send, recv_sem=recv, device_id=device, device_id_type=MESH
    )


def synth_kernel(
    lmax, circle_total, line, order_size, orders, csims,
    m_ref, r_ref, line_ref, e_ref, p_ref, out_ref,
    held, land, tab, acc, own, ysend, yrecv, asend, lens, ltab, lpart, csend, crecv,
    zs, zr, ys, yr, as_, ar, ls, lr, cs, cr,
):
    order_pos, blk, h, y, pair, peers = neighbours(order_size, line)
    rows = e_ref.shape[1]
    circles = r_ref.shape[0] // 2
    part = circles // order_size
    amplitude = math.sqrt(2.0 / lmax)
    colat = 2 * r_ref[...] + 1

    def along(src, block, o, way):
        return remote(
            src, held.at[block, o], zs.at[way, block, o], zr.at[block, o], {"blk": blk - 2 + 4 * way}
        )

    def send_own(o):
        @pl.when(h > 0)
        def _():
            along(e_ref.at[o], h, o, 0).start()

        @pl.when(h < line - 1)
        def _():
            along(e_ref.at[o], h, o, 1).start()

    def across(o):
        return remote(ysend.at[o], yrecv.at[o], ys.at[o], yr.at[o], {"blk": pair})

    def spread(o, peer, source):
        begin = pl.multiple_of(peer * part, part)
        return remote(
            asend.at[o, pl.ds(begin, part)], land.at[source * orders + o],
            as_.at[peer, o], ar.at[source, o], {"order": peer},
        )

    def share(o, lane):
        begin = pl.multiple_of(lane * rows, rows)
        return remote(
            p_ref.at[o], lens.at[o, pl.ds(begin, rows)], ls.at[o], lr.at[o], {"blk": pair}
        )

    def chain(way, target, o):
        return remote(
            csend.at[way, target, o], crecv.at[way, target, o],
            cs.at[way, target, o], cr.at[way, target, o], {"blk": blk - 2 + 4 * way},
        )

    greet(order_size, line)
    for o in range(orders):
        share(o, y).start()
        send_own(o)
    lens[:, pl.ds(pl.multiple_of(y * rows, rows), rows), :] = p_ref[...]

    def make_table(block, carry):
        degree = (2 * block + y) * rows + lax.broadcasted_iota(jnp.int32, (1, rows), 1)
        freq = 2 * degree + 1
        sine, cosine = sin_cos(colat * freq, 8 * circle_total)
        sine, cosine = sine * amplitude, cosine * amplitude
        weight = freq.astype(F32) / (2.0 * lmax)
        for k, value in enumerate((cosine, sine, cosine * weight, sine * weight)):
            tab[block, 2 * k * circles : 2 * (k + 1) * circles, :] = value.astype(BF)
        return carry

    def make_lens_table(target, carry):
        degree = 2 * h * rows + lax.broadcasted_iota(jnp.int32, (1, 2 * rows), 1)
        freq = 2 * degree + 1
        sine, cosine = sin_cos((2 * line_ref[target] + 1) * freq, 8 * circle_total)
        sine, cosine = sine * amplitude, cosine * amplitude
        weight = freq.astype(F32) / (2.0 * lmax)
        for k, value in enumerate((cosine, sine, sine * weight, cosine * weight)):
            ltab[k, target] = value.astype(BF)
        return carry

    lax.fori_loop(0, line, make_lens_table, 0)
    lax.fori_loop(0, line, make_table, 0)
    ps, pc = sin_cos(colat * 2, 8 * circle_total)
    kappa = 2.0 / (2.0 * lmax)

    def product(values, block, o):
        degree = (2 * block + y) * rows + lax.broadcasted_iota(jnp.int32, values.shape, 0)
        values = jnp.where(degree >= m_ref[o], values, jnp.zeros_like(values))
        return jnp.dot(tab[block], values, preferred_element_type=F32)

    def finish(o):
        across(o).wait_recv()
        cut = 4 * csims
        asend[o, :, :cut] = (own[o] + yrecv[o].astype(F32)).astype(BF)
        asend[o, :, cut:] = lpart[o, h].astype(BF)
        for peer in peers:
            spread(o, peer, order_pos).start()
        begin = pl.multiple_of(order_pos * part, part)
        land[order_pos * orders + o] = asend[o, pl.ds(begin, part)]

    def lens_sums(o):
        share(o, 1 - y).wait_recv()
        m = m_ref[o]
        cm, sm = quarter_turns(m)
        values = lens[o]
        degree = 2 * h * rows + lax.broadcasted_iota(jnp.int32, values.shape, 0)
        values = jnp.where(degree >= m, values, jnp.zeros_like(values))
        flat, split = (line * circles, 2 * rows), (line, circles, csims)
        theta = jnp.dot(ltab[2 + (m & 1)].reshape(flat), values, preferred_element_type=F32)
        lpart[o, :, :, :csims] = ((sm - cm) * theta).reshape(split)
        flow = jnp.dot(ltab[m & 1].reshape(flat), values, preferred_element_type=F32)
        lpart[o, :, :, csims:] = ((cm + sm) * (m.astype(F32) * (1.0 / lmax)) * flow).reshape(split)

    def stage(t, o):
        def leftward(target, carry):
            @pl.when((target <= h) & (h < line - 1))
            def _():
                chain(0, target, o).wait_recv()
                lpart[o, target] += crecv[0, target, o].astype(F32)

            @pl.when(target < h)
            def _():
                csend[0, target, o] = lpart[o, target].astype(BF)
                chain(0, target, o).start()

            return carry

        def rightward(target, carry):
            @pl.when((target >= h) & (h > 0))
            def _():
                chain(1, target, o).wait_recv()
                lpart[o, target] += crecv[1, target, o].astype(F32)

            @pl.when(target > h)
            def _():
                csend[1, target, o] = lpart[o, target].astype(BF)
                chain(1, target, o).start()

            return carry

        @pl.when(h == line - 1 - t)
        def _():
            lax.fori_loop(0, line, leftward, 0)

        @pl.when(h == t)
        def _():
            lax.fori_loop(0, line, rightward, 0)

    def hop(s, o):
        after, before = h + s, h - s

        @pl.when(after < line)
        def _():
            along(held.at[after, o], after, o, 0).wait_recv()

            @pl.when(h > 0)
            def _():
                along(held.at[after, o], after, o, 0).start()

        @pl.when(before >= 0)
        def _():
            along(held.at[before, o], before, o, 1).wait_recv()

            @pl.when(h < line - 1)
            def _():
                along(held.at[before, o], before, o, 1).start()

        @pl.when(after < line)
        def _():
            acc[o] += product(held[after, o], after, o)

        @pl.when(before >= 0)
        def _():
            acc[o] += product(held[before, o], before, o)

    def emode_maps(o):
        cm, sm = quarter_turns(m_ref[o])
        factor = m_ref[o].astype(F32) * (1.0 / lmax)
        c0, s0, gc0, gs0 = (acc[o, 2 * k * circles : 2 * (k + 1) * circles] for k in range(4))
        a, b = cm * c0 + sm * s0, cm * s0 - sm * c0
        gc, gs = cm * gc0 + sm * gs0, cm * gs0 - sm * gc0
        maps = (
            -(pc * (gs + kappa * b) + ps * (gc + kappa * a)),
            -(pc * (gs - kappa * b) - ps * (gc - kappa * a)),
            factor * (pc * a - ps * b),
            factor * (pc * a + ps * b),
        )
        for k, value in enumerate(maps):
            at = slice(k * csims, (k + 1) * csims)
            own[o, :, at] = value[:circles]
            ysend[o, :, at] = value[circles:].astype(BF)
        across(o).start()

    def one_phase(s, outer):
        def one_order(o, carry):
            @pl.when(s < line)
            def _():
                hop(s, o)

            @pl.when(s == 1)
            def _():
                lens_sums(o)

            @pl.when(s == line - 1)
            def _():
                emode_maps(o)

            stage(s - 1, o)

            @pl.when(s == line)
            def _():
                finish(o)

            return carry

        return lax.fori_loop(0, orders, one_order, outer)

    def own_product(o, carry):
        acc[o] = product(e_ref[o], h, o)
        return carry

    lax.fori_loop(0, orders, own_product, 0)
    lax.fori_loop(1, line + 1, one_phase, 0)

    def settle(o, carry):
        across(o).wait_send()
        share(o, y).wait_send()
        for peer in peers:
            spread(o, peer, order_pos).wait_send()
            spread(o, peer, peer).wait_recv()

        def sent(block, inner):
            @pl.when((h > 0) & (block >= h))
            def _():
                along(held.at[block, o], block, o, 0).wait_send()

            @pl.when((h < line - 1) & (block <= h))
            def _():
                along(held.at[block, o], block, o, 1).wait_send()

            @pl.when(block < h)
            def _():
                chain(0, block, o).wait_send()

            @pl.when(block > h)
            def _():
                chain(1, block, o).wait_send()

            return inner

        lax.fori_loop(0, line, sent, 0)
        return carry

    lax.fori_loop(0, orders, settle, 0)
    out_ref[...] = land[...]


def pixel_kernel(orders, csims, par_ref, w_ref, m_ref, f_ref, ft_ref, out_ref):
    count = m_ref.shape[0]
    sims = csims // 2
    low = lax.broadcasted_iota(jnp.int32, (orders, csims), 1) < sims
    begin = pl.program_id(0) * count

    def halves(x, y):
        first = jnp.where(low, x, pltpu.roll(y, sims, 1))
        second = jnp.where(low, pltpu.roll(x, sims, 1), y)
        return first, second

    for c in range(count):
        qt, ut, qc, uc, dt, dc = (
            m_ref[c, :, k * csims : (k + 1) * csims].astype(F32) for k in range(6)
        )
        t_re, t_im = halves(qt, ut)
        c_re, c_im = halves(qc, uc)
        dt_re, dt_im = halves(dt, dt)
        dc_re, dc_im = halves(dc, dc)
        real = jnp.concatenate([t_re, -c_im, dt_re, -dc_im], axis=1)
        imag = jnp.concatenate([t_im, c_re, dt_im, dc_re], axis=1)
        arranged = jnp.concatenate([real, imag], axis=0).astype(BF)
        parity = par_ref[begin + c]
        pixels = jnp.dot(ft_ref[parity], arranged, preferred_element_type=F32)
        deflected = (
            pixels[:, 2 * csims : 3 * csims] * pixels[:, :csims]
            + pixels[:, 3 * csims :] * pixels[:, csims : 2 * csims]
        ).astype(BF)
        analysed = jnp.dot(f_ref[parity], deflected, preferred_element_type=F32) * w_ref[begin + c]
        gq, gu = halves(analysed[:orders], analysed[orders:])
        out_ref[c, :, :csims] = gq.astype(BF)
        out_ref[c, :, csims:] = gu.astype(BF)


def adjoint_kernel(
    lmax, circle_total, line, order_size, orders, csims,
    m_ref, r_ref, rc_ref, w_ref, grad_ref, curl_ref,
    gath, tab, acc, zs, zr, ys, yr, as_, ar,
):
    order_pos, blk, h, y, pair, peers = neighbours(order_size, line)
    degrees = grad_ref.shape[0]
    circles = gath.shape[2]
    part = w_ref.shape[1]
    amplitude = math.sqrt(2.0 / lmax)

    def back(peer, source):
        begin = pl.multiple_of(source * part, part)
        return remote(
            w_ref.at[pl.ds(peer * orders, orders)], gath.at[blk, :, pl.ds(begin, part)],
            as_.at[peer], ar.at[source], {"order": peer},
        )

    def along(line_at, way):
        block = gath.at[2 * line_at + y]
        return remote(block, block, zs.at[way, line_at], zr.at[line_at], {"blk": blk - 2 + 4 * way})

    def across(line_at, lane):
        block = gath.at[2 * line_at + lane]
        return remote(block, block, ys.at[line_at], yr.at[line_at], {"blk": pair})

    greet(order_size, line)
    for peer in peers:
        back(peer, order_pos).start()
    begin = pl.multiple_of(order_pos * part, part)
    gath[blk, :, pl.ds(begin, part), :] = w_ref[pl.ds(order_pos * orders, orders)]

    def make_table(block, carry):
        degree = blk * degrees + lax.broadcasted_iota(jnp.int32, (degrees, 1), 0)
        sine, cosine = sin_cos((2 * degree + 1) * (2 * r_ref[block] + 1), 8 * circle_total)
        tab[block, :, :circles] = (cosine * amplitude).astype(BF)
        tab[block, :, circles:] = (sine * amplitude).astype(BF)
        return carry

    lax.fori_loop(0, line // 2, make_table, 0)

    def add(block):
        ps, pc = sin_cos(2 * (2 * rc_ref[block] + 1), 8 * circle_total)
        ups, vps = [], []
        for o in range(orders):
            cm, sm = quarter_turns(m_ref[o])
            gq = gath[block, o, :, :csims].astype(F32)
            gu = gath[block, o, :, csims:].astype(F32)
            x1, y1 = pc * (gq + gu), ps * (gq - gu)
            x2, y2 = pc * (gu - gq), ps * (gu + gq)
            ups += [(cm * x1 + sm * y1).astype(BF), (cm * x2 + sm * y2).astype(BF)]
            vps += [(sm * x1 - cm * y1).astype(BF), (sm * x2 - cm * y2).astype(BF)]
        values = jnp.concatenate(
            [jnp.concatenate(ups, axis=1), jnp.concatenate(vps, axis=1)], axis=0
        )
        acc[...] += jnp.dot(tab[block], values, preferred_element_type=F32)

    for peer in peers:
        back(peer, peer).wait_recv()

    @pl.when(h > 0)
    def _():
        along(h, 0).start()

    @pl.when(h < line - 1)
    def _():
        along(h, 1).start()

    across(h, y).start()
    lax.fori_loop(line // 2, 2 * line, make_table, 0)
    acc[...] = jnp.zeros_like(acc)

    def hop(s, carry):
        after, before = h + s, h - s

        @pl.when((s > 0) & (after < line))
        def _():
            along(after, 0).wait_recv()

            @pl.when(h > 0)
            def _():
                along(after, 0).start()

            across(after, y).start()

        @pl.when((s > 0) & (before >= 0))
        def _():
            along(before, 1).wait_recv()

            @pl.when(h < line - 1)
            def _():
                along(before, 1).start()

            across(before, y).start()

        @pl.when(after < line)
        def _():
            add(2 * after + y)

        @pl.when((s > 0) & (before >= 0))
        def _():
            add(2 * before + y)

        return carry

    lax.fori_loop(0, line, hop, 0)

    def cross(s, carry):
        after, before = h + s, h - s

        @pl.when(after < line)
        def _():
            across(after, 1 - y).wait_recv()
            add(2 * after + 1 - y)

        @pl.when((s > 0) & (before >= 0))
        def _():
            across(before, 1 - y).wait_recv()
            add(2 * before + 1 - y)

        return carry

    lax.fori_loop(0, line, cross, 0)
    for peer in peers:
        back(peer, order_pos).wait_send()

    def settle(line_at, carry):
        across(line_at, y).wait_send()

        @pl.when((h > 0) & (line_at >= h))
        def _():
            along(line_at, 0).wait_send()

        @pl.when((h < line - 1) & (line_at <= h))
        def _():
            along(line_at, 1).wait_send()

        return carry

    lax.fori_loop(0, line, settle, 0)
    rows = blk * degrees + lax.broadcasted_iota(jnp.int32, (degrees, csims), 0)
    for o in range(orders):
        inside = rows >= m_ref[o]
        at = slice(o * csims, (o + 1) * csims)
        grad = acc[:, 2 * o * csims : (2 * o + 1) * csims]
        curl = acc[:, (2 * o + 1) * csims : (2 * o + 2) * csims]
        grad_ref[:, at] = jnp.where(inside, grad, 0.0).astype(BF)
        curl_ref[:, at] = jnp.where(inside, curl, 0.0).astype(BF)


def longitude_table(lmax, parity, order_list):
    full_circle = 2 * lmax
    longitude = jnp.arange(LONGS, dtype=jnp.int32)
    phase_steps = order_list[None, :, None] * (2 * longitude[None, None, :] + parity[:, None, None])
    phase_steps = jnp.mod(phase_steps, 2 * full_circle)
    angles = phase_steps.astype(jnp.float32) * (math.pi / full_circle)
    scaling = 1.0 / math.sqrt(order_list.shape[0])
    fourier = jnp.concatenate([jnp.cos(angles) * scaling, -jnp.sin(angles) * scaling], axis=1)
    return fourier.astype(BF)


def divisor(total, limit):
    return next(k for k in range(min(total, limit), 0, -1) if total % k == 0)


SMEM = pl.BlockSpec(memory_space=pltpu.SMEM)
VMEM = pl.BlockSpec(memory_space=pltpu.VMEM)
PARAMS = pltpu.CompilerParams(vmem_limit_bytes=48 << 20)


def body(order_size, blk_size, emode_coeffs, lensing_coeffs, order_values, circle_indices, circle_weights):
    degree_local, orders, csims = emode_coeffs.shape
    lmax = degree_local * blk_size
    circle_total = circle_indices.shape[0]
    order_total = order_values.shape[0]
    circles = circle_total // blk_size
    order_pos = lax.axis_index("order")
    block_pos = lax.axis_index("blk")
    my_orders = lax.dynamic_slice_in_dim(order_values, order_pos * orders, orders)
    width = orders * csims
    line = blk_size // 2
    blocks = circle_indices.reshape(blk_size, circles)
    pair_circles = jnp.concatenate(
        [
            lax.dynamic_index_in_dim(blocks, block_pos, 0, keepdims=False),
            lax.dynamic_index_in_dim(blocks, block_pos ^ 1, 0, keepdims=False),
        ]
    )
    line_circles = lax.dynamic_index_in_dim(
        circle_indices.reshape(line, 2, circles), block_pos % 2, 1, keepdims=False
    )
    fourier = longitude_table(lmax, jnp.arange(2, dtype=jnp.int32), order_values)
    fourier_t = fourier.transpose(0, 2, 1)
    part = circles // order_size
    dma = pltpu.SemaphoreType.DMA
    spread = pl.pallas_call(
        functools.partial(synth_kernel, lmax, circle_total, line, order_size, orders, csims),
        out_shape=jax.ShapeDtypeStruct((order_total, part, 6 * csims), BF),
        in_specs=[SMEM, VMEM, VMEM, VMEM, VMEM],
        out_specs=VMEM,
        scratch_shapes=[
            pltpu.VMEM((line, orders, degree_local, csims), BF),
            pltpu.VMEM((order_total, part, 6 * csims), BF),
            pltpu.VMEM((line, 8 * circles, degree_local), BF),
            pltpu.VMEM((orders, 8 * circles, csims), F32),
            pltpu.VMEM((orders, circles, 4 * csims), F32),
            pltpu.VMEM((orders, circles, 4 * csims), BF),
            pltpu.VMEM((orders, circles, 4 * csims), BF),
            pltpu.VMEM((orders, circles, 6 * csims), BF),
            pltpu.VMEM((orders, 2 * degree_local, csims), BF),
            pltpu.VMEM((4, line, circles, 2 * degree_local), BF),
            pltpu.VMEM((orders, line, circles, 2 * csims), F32),
            pltpu.VMEM((2, line, orders, circles, 2 * csims), BF),
            pltpu.VMEM((2, line, orders, circles, 2 * csims), BF),
            dma((2, line, orders)),
            dma((line, orders)),
            dma((orders,)),
            dma((orders,)),
            dma((order_size, orders)),
            dma((order_size, orders)),
            dma((orders,)),
            dma((orders,)),
            dma((2, line, orders)),
            dma((2, line, orders)),
        ],
        compiler_params=pltpu.CompilerParams(
            vmem_limit_bytes=48 << 20, collective_id=0, has_side_effects=True
        ),
        name="synth",
    )(
        my_orders,
        pair_circles[:, None],
        line_circles[:, :, None],
        emode_coeffs.transpose(1, 0, 2),
        lensing_coeffs.transpose(1, 0, 2),
    )
    spread = spread.transpose(1, 0, 2)
    begin = block_pos * circles + order_pos * part
    part_circles = lax.dynamic_slice_in_dim(circle_indices, begin, part)
    part_weights = lax.dynamic_slice_in_dim(circle_weights, begin, part)
    count = divisor(part, 8)
    weighted = pl.pallas_call(
        functools.partial(pixel_kernel, order_total, csims),
        out_shape=jax.ShapeDtypeStruct((part, order_total, 2 * csims), BF),
        grid=(part // count,),
        in_specs=[
            SMEM,
            SMEM,
            pl.BlockSpec((count, order_total, 6 * csims), lambda i: (i, 0, 0)),
            pl.BlockSpec((2, 2 * order_total, LONGS), lambda i: (0, 0, 0)),
            pl.BlockSpec((2, LONGS, 2 * order_total), lambda i: (0, 0, 0)),
        ],
        out_specs=pl.BlockSpec((count, order_total, 2 * csims), lambda i: (i, 0, 0)),
        compiler_params=PARAMS,
        name="pixels",
    )(jnp.mod(part_circles, 2), part_weights, spread, fourier, fourier_t)
    grad, curl = pl.pallas_call(
        functools.partial(adjoint_kernel, lmax, circle_total, line, order_size, orders, csims),
        out_shape=[jax.ShapeDtypeStruct((degree_local, width), BF)] * 2,
        in_specs=[SMEM, VMEM, VMEM, VMEM],
        out_specs=[VMEM, VMEM],
        scratch_shapes=[
            pltpu.VMEM((blk_size, orders, circles, 2 * csims), BF),
            pltpu.VMEM((blk_size, degree_local, 2 * circles), BF),
            pltpu.VMEM((degree_local, 2 * width), F32),
            dma((2, line)),
            dma((line,)),
            dma((line,)),
            dma((line,)),
            dma((order_size,)),
            dma((order_size,)),
        ],
        compiler_params=pltpu.CompilerParams(
            vmem_limit_bytes=48 << 20, collective_id=1, has_side_effects=True
        ),
        name="adjoint",
    )(my_orders, blocks[:, None, :], blocks[:, :, None], weighted.transpose(1, 0, 2))
    return grad.reshape(emode_coeffs.shape), curl.reshape(emode_coeffs.shape)


def solution(mesh):
    in_specs = (P("blk", "order", None), P("blk", "order", None), P(), P(), P())
    out_specs = (P("blk", "order", None), P("blk", "order", None))
    sizes = (mesh.shape["order"], mesh.shape["blk"])
    return jax.shard_map(
        functools.partial(body, *sizes), mesh=mesh, in_specs=in_specs, out_specs=out_specs, check_vma=False
    )
```

profile of v0, /device:TPU:0, one launch (start us, length us, event | category | flops | bytes accessed | tf_op | source)
XLA Modules:
  0.0 108.3 jit_solution(13102429428645960490)
XLA Ops:
  0.6 0.0 copy-start
  0.7 0.7 copy-done
  1.3 0.1 copy.23.line_ref
  1.5 0.1 copy.22.r_ref
  1.7 0.0 copy-start.1
  1.7 0.6 copy-done.1
  2.3 0.1 dynamic_slice.20.m_ref
  2.4 1.3 %copy_bitcast_fusion.1 = (bf16[4,512,128]{2,1,0:T(8,128)(2,1)S(1)}, bf16[4,512,128]{2,1,0:T(8,128)(2,1)S(1)}) fusion(bf16[512,4,128]{2,1,0:T(4,128)(2,1)} %param.6, bf16[512,4,128]{2,1,0:T(4,128)(2,1)} %param.5), kind=kLoop, calls=%fused_computation.1 | loop fusion | bytes 2097152 | tf_op jit(solution)/shard_map/transpose | solution.py:599
  3.8 55.0 %synth.1 = bf16[16,32,768]{2,1,0:T(8,128)(2,1)S(1)} custom-call(s32[4]{0:T(128)S(1)} %dynamic_slice.20.m_ref, s32[256,1]{1,0:T(8,128)S(1)} %copy.22.r_ref, s32[4,128,1]{2,1,0:T(8,128)S(1)} %copy.23.line_ref, bf16[4,512,128]{2,1,0:T(8,128)(2,1)S(1)} %get-tuple-element.11.e_ref, bf16[4,512,128]{2,1,0:T(8,128)(2,1)S(1)} %get-tuple-element.10.p_ref), custom_call_target="tpu_custom_call" | custom-call | tf_op jit(solution)/shard_map/synth/pallas_call | solution.py:560
  58.8 0.4 copy.32
  59.2 0.1 and_select_fusion.par_ref
  59.3 0.8 dynamic_slice.22.w_ref
  60.1 0.2 multiply_convert_fusion.1
  60.3 0.1 copy.25
  60.4 7.9 %pixels.1 = bf16[32,16,256]{2,1,0:T(8,128)(2,1)S(1)} custom-call(s32[32]{0:T(128)S(1)} %and_select_fusion.par_ref, f32[32]{0:T(128)S(1)} %dynamic_slice.22.w_ref, bf16[32,16,768]{2,1,0:T(8,128)(2,1)S(1)} %bitcast.21, bf16[2,32,256]{2,1,0:T(8,128)(2,1)S(1)} %pad_maximum_fusion.f_ref, bf16[2,256,32]{2,1,0:T(8,128)(2,1)S(1)} %bitcast.23), custom_call_target="tpu_custom_call" | custom-call | tf_op jit(solution)/shard_map/pixels/pallas_call | solution.py:606
  68.4 0.1 copy.33
  68.4 0.2 copy.27.rc_ref
  68.7 37.8 %adjoint.1 = (bf16[512,512]{1,0:T(8,128)(2,1)S(1)}, bf16[512,512]{1,0:T(8,128)(2,1)S(1)}) custom-call(s32[4]{0:T(128)S(1)} %dynamic_slice.20.m_ref, s32[8,1,128]{2,1,0:T(1,128)S(1)} %bitcast.27, s32[8,128,1]{2,1,0:T(8,128)S(1)} %copy.27.rc_ref, bf16[16,32,256]{2,1,0:T(8,128)(2,1)S(1)} %bitcast.22), custom_call_target="tpu_custom_call" | custom-call | tf_op jit(solution)/shard_map/adjoint/pallas_call | solution.py:621
  106.5 0.9 reshape.47
  107.4 0.9 reshape.48
  (6 shorter events, 0.0 us)
Async XLA Ops:
  0.6 0.7 copy-start
  1.7 0.7 copy-start.1
where the time goes:
time: 109 us; the launch traced here: 108 us
  Pallas kernels  101 us (93%)
  local copies, waits for them, and re-layouts  6.49 us (6%)
    pallas_call x1, Pallas kernels, body(): pl.pallas_call(functools.partial(synth_kernel, lmax, circle_total, line,...  55 us
    pallas_call x1, Pallas kernels, body(): pl.pallas_call(functools.partial(adjoint_kernel, lmax, circle_total, line...  37.8 us
    pallas_call x1, Pallas kernels, body(): pl.pallas_call(functools.partial(pixel_kernel, order_total, csims), out_s...  7.93 us

commit v1 on v0

--- a/solution.py
+++ b/solution.py
@@ -532,7 +532,7 @@
 PARAMS = pltpu.CompilerParams(vmem_limit_bytes=48 << 20)
 
 
-def body(order_size, blk_size, emode_coeffs, lensing_coeffs, order_values, circle_indices, circle_weights):
+def by_circle(order_size, blk_size, emode_coeffs, lensing_coeffs, order_values, circle_indices, circle_weights):
     degree_local, orders, csims = emode_coeffs.shape
     lmax = degree_local * blk_size
     circle_total = circle_indices.shape[0]
@@ -642,6 +642,364 @@
     return grad.reshape(emode_coeffs.shape), curl.reshape(emode_coeffs.shape)
 
 
+def turned(dims, left, right):
+    return lax.dot_general(left, right, (dims, ((), ())), preferred_element_type=F32)
+
+
+def realization_kernel(
+    lmax, circle_total, order_size, blk_size, orders, csims, group,
+    em_ref, le_ref, m_ref, ci_ref, cw_ref, grad_ref, curl_ref,
+    pick, out1, land1, out2, land2, tab, xs, maps, waves, waves_t, ana, pairs, wlane,
+    s1, r1, s2, r2,
+):
+    order_pos, blk = lax.axis_index("order"), lax.axis_index("blk")
+    devices = order_size * blk_size
+    me = order_pos * blk_size + blk
+    degrees = em_ref.shape[0]
+    half = degrees // 2
+    sims = csims // 2
+    low = blk_size // 2
+    span = low * half
+    couples = circle_total // 2
+    quarter = couples // 2
+    rows = order_size * 2 * orders
+    tile = 2 * orders
+    full = 8 * circle_total
+    width = orders * csims
+
+    def peer(k):
+        to_order = lax.rem(order_pos + (order_size - 1) - lax.rem(k, order_size), order_size)
+        to_blk = lax.rem(blk + (blk_size - 1) - lax.div(k, order_size), blk_size)
+        return to_order, to_blk
+
+    def hand(src, dst, send, recv, s, k):
+        o, b = peer(k)
+        return pltpu.make_async_remote_copy(
+            src_ref=src.at[s, o, b], dst_ref=dst.at[s, order_pos, blk],
+            send_sem=send.at[s, o, b], recv_sem=recv.at[s, order_pos, blk],
+            device_id={"order": o, "blk": b}, device_id_type=MESH,
+        )
+
+    def arrival(src, dst, send, recv, s, k):
+        o, b = peer(k)
+        return pltpu.make_async_remote_copy(
+            src_ref=src.at[s, o, b], dst_ref=dst.at[s, o, b],
+            send_sem=send.at[s, o, b], recv_sem=recv.at[s, o, b],
+            device_id={"order": o, "blk": b}, device_id_type=MESH,
+        )
+
+    first = (out1, land1, s1, r1)
+    second = (out2, land2, s2, r2)
+
+    def send_all(args, s):
+        def one(k, carry):
+            hand(*args, s, k).start()
+            return carry
+
+        lax.fori_loop(0, devices - 1, one, 0)
+
+    def await_all(args, s):
+        def one(k, carry):
+            arrival(*args, s, k).wait_recv()
+            return carry
+
+        lax.fori_loop(0, devices - 1, one, 0)
+
+    def sent_all(args, s):
+        def one(k, carry):
+            hand(*args, s, k).wait_send()
+            return carry
+
+        lax.fori_loop(0, devices - 1, one, 0)
+
+    barrier = pltpu.get_barrier_semaphore()
+
+    def greet_one(k, carry):
+        o, b = peer(k)
+        pl.semaphore_signal(barrier, inc=1, device_id={"order": o, "blk": b}, device_id_type=MESH)
+        return carry
+
+    lax.fori_loop(0, devices - 1, greet_one, 0)
+
+    def arrange(s):
+        row = lax.broadcasted_iota(jnp.int32, (devices * tile, 1), 0)
+        within = lax.rem(row, tile)
+        column = (
+            lax.rem(within, orders) * csims + lax.div(within, orders) * sims + lax.div(row, tile) * group + s
+        )
+        lane = lax.broadcasted_iota(jnp.int32, (devices * tile, width), 1)
+        choice = jnp.where(lane == column, 1.0, 0.0).astype(BF)
+        pick[s] = choice
+        split = (devices, tile, degrees)
+        e = turned(((1,), (1,)), choice, em_ref[...]).reshape(split)
+        p = turned(((1,), (1,)), choice, le_ref[...]).reshape(split)
+        both = jnp.concatenate([e, p], axis=1).astype(BF)
+        out1[s] = both.reshape(order_size, blk_size, 2 * tile, degrees)
+        land1[s, order_pos, blk] = out1[s, order_pos, blk]
+
+    for s in range(group):
+        arrange(s)
+        if s == 0:
+            pl.semaphore_wait(barrier, devices - 1)
+        send_all(first, s)
+
+    amplitude = math.sqrt(2.0 / lmax)
+    chunk = 64
+
+    def make_table(i, carry):
+        begin = pl.multiple_of(i * chunk, chunk)
+        q = i * chunk + lax.broadcasted_iota(jnp.int32, (chunk, 1), 0)
+        colat = 2 * (2 * lax.rem(q, quarter) + lax.div(q, quarter)) + 1
+        step = 4 * lax.broadcasted_iota(jnp.int32, (1, half), 1)
+        sb, cb = sin_cos(colat * step, full)
+        k = lax.broadcasted_iota(jnp.int32, (1, 128), 1)
+        start = 2 * degrees * lax.rem(k, low) + 2 * lax.div(k, low) + 1
+        sa, ca = sin_cos(colat * start, full)
+        sa, ca = sa * amplitude, ca * amplitude
+        for n in range(2 * low):
+            at = slice(n * half, (n + 1) * half)
+            s0, c0 = sa[:, n : n + 1], ca[:, n : n + 1]
+            tab[pl.ds(begin, chunk), at] = (c0 * cb - s0 * sb).astype(BF)
+            tab[pl.ds(couples + begin, chunk), at] = (s0 * cb + c0 * sb).astype(BF)
+        return carry
+
+    lax.fori_loop(0, couples // chunk, make_table, 0)
+
+    row = lax.broadcasted_iota(jnp.int32, (rows, 1), 0)
+    slot = lax.div(row, tile) * orders + lax.rem(row, orders)
+    imaginary = lax.rem(lax.div(row, orders), 2) == 1
+    order_total = m_ref.shape[1]
+    slots = lax.broadcasted_iota(jnp.int32, (rows, order_total), 1)
+    m = jnp.sum(
+        jnp.where(slots == slot, m_ref[...].astype(F32), 0.0), axis=1, keepdims=True
+    ).astype(jnp.int32)
+    cm, sm = quarter_turns(m)
+    factor = m.astype(F32) * (1.0 / lmax)
+
+    lane = lax.broadcasted_iota(jnp.int32, (1, circle_total), 1)
+    at_couple = lax.rem(lane, couples)
+    near = 2 * lax.rem(at_couple, quarter) + lax.div(at_couple, quarter)
+    circle = jnp.where(lane < couples, near, circle_total - 1 - near)
+    ps, pc = sin_cos(2 * (2 * circle + 1), full)
+
+    index_t = ci_ref[...].astype(F32).T
+    weight_t = cw_ref[...].T
+    circle_f = circle.astype(F32)
+    total = jnp.zeros((8, circle_total), F32)
+    for k in range(ci_ref.shape[0]):
+        for g in range(ci_ref.shape[1] // 8):
+            at = slice(8 * g, 8 * g + 8)
+            total += jnp.where(index_t[at, k : k + 1] == circle_f, weight_t[at, k : k + 1], 0.0)
+    wlane[...] = jnp.sum(total, axis=0, keepdims=True)
+
+    scaling = 1.0 / math.sqrt(order_total)
+    turn = 2 * lmax
+    longitude = lax.broadcasted_iota(jnp.int32, (1, LONGS), 1)
+    for parity in range(2):
+        si, co = sin_cos(m * (2 * longitude + parity), 2 * turn)
+        si, co = si * scaling, co * scaling
+        straight = jnp.where(imaginary, -si, co)
+        crossed = jnp.where(imaginary, -co, -si)
+        waves_t[parity] = straight.astype(BF)
+        waves[parity, 0] = straight.T.astype(BF)
+        waves[parity, 1] = crossed.T.astype(BF)
+
+    kappa = 2.0 / (2.0 * lmax)
+    within_deg = lax.broadcasted_iota(jnp.int32, (1, degrees), 1)
+    within_deg = 2 * lax.rem(within_deg, half) + lax.div(within_deg, half)
+
+    def process(s, carry):
+        await_all(first, s)
+
+        def fold(b, inner):
+            deg = b * degrees + within_deg
+            far = deg + low * degrees
+            wd = (2 * deg + 1).astype(F32) * (1.0 / (2.0 * lmax))
+            wf = (2 * far + 1).astype(F32) * (1.0 / (2.0 * lmax))
+            one, two = land1[s, :, b].astype(F32), land1[s, :, b + low].astype(F32)
+            for k in range(2):
+                x = one[:, k * tile : (k + 1) * tile].reshape(rows, degrees)
+                z = two[:, k * tile : (k + 1) * tile].reshape(rows, degrees)
+                x = jnp.where(deg >= m, x, 0.0)
+                z = jnp.where(far >= m, z, 0.0)
+                flat, steep = (x - z).astype(BF), (wd * x - wf * z).astype(BF)
+                for parity in range(2):
+                    to = pl.ds(pl.multiple_of(parity * span + b * half, half), half)
+                    of = slice(parity * half, (parity + 1) * half)
+                    xs[2 * k * rows : (2 * k + 1) * rows, to] = flat[:, of]
+                    xs[(2 * k + 1) * rows : (2 * k + 2) * rows, to] = steep[:, of]
+            return inner
+
+        lax.fori_loop(0, low, fold, 0)
+        even = turned(((1,), (1,)), xs[:, :span], tab[:, :span])
+        odd = turned(((1,), (1,)), xs[:, span:], tab[:, span:])
+        plus, minus = even + odd, even - odd
+        c_all = jnp.concatenate([plus[:, :couples], minus[:, couples:]], axis=1)
+        s_all = jnp.concatenate([plus[:, couples:], minus[:, :couples]], axis=1)
+
+        def turns(k):
+            at = slice(k * rows, (k + 1) * rows)
+            c0, s0 = c_all[at], s_all[at]
+            return cm * c0 + sm * s0, cm * s0 - sm * c0
+
+        a, b = turns(0)
+        gc, gs = turns(1)
+        la, _ = turns(2)
+        _, lgs = turns(3)
+        maps[0] = (-(pc * (gs + kappa * b) + ps * (gc + kappa * a))).astype(BF)
+        maps[1] = (-(pc * (gs - kappa * b) - ps * (gc - kappa * a))).astype(BF)
+        maps[2] = (-lgs).astype(BF)
+        maps[3] = (factor * (pc * a - ps * b)).astype(BF)
+        maps[4] = (factor * (pc * a + ps * b)).astype(BF)
+        maps[5] = (factor * la).astype(BF)
+
+        def pixels(n, inner):
+            at = pl.ds(pl.multiple_of(n * quarter, quarter), quarter)
+            parity = lax.rem(n + lax.div(n, 2), 2)
+            qt, ut, dt = (
+                jnp.dot(waves[parity, 0], maps[k, :, at], preferred_element_type=F32) for k in range(3)
+            )
+            qp, up, dp = (
+                jnp.dot(waves[parity, 1], maps[k, :, at], preferred_element_type=F32) for k in range(3, 6)
+            )
+            dq = (dt * qt + dp * qp).astype(BF)
+            du = (dt * ut + dp * up).astype(BF)
+            w = wlane[:, at]
+            ana[0, :, at] = (jnp.dot(waves_t[parity], dq, preferred_element_type=F32) * w).astype(BF)
+            ana[1, :, at] = (jnp.dot(waves_t[parity], du, preferred_element_type=F32) * w).astype(BF)
+            return inner
+
+        lax.fori_loop(0, 4, pixels, 0)
+        gq, gu = ana[0].astype(F32), ana[1].astype(F32)
+        x1, y1 = pc * (gq + gu), ps * (gq - gu)
+        x2, y2 = pc * (gu - gq), ps * (gu + gq)
+        for k, (x, y) in enumerate(((x1, y1), (x2, y2))):
+            at = slice(k * rows, (k + 1) * rows)
+            up, vp = cm * x + sm * y, sm * x - cm * y
+            near_u, far_u = up[:, :couples], up[:, couples:]
+            near_v, far_v = vp[:, :couples], vp[:, couples:]
+            pairs[0, at, :couples] = (near_u + far_v).astype(BF)
+            pairs[0, at, couples:] = (near_v + far_u).astype(BF)
+            pairs[1, at, :couples] = (near_u - far_v).astype(BF)
+            pairs[1, at, couples:] = (near_v - far_u).astype(BF)
+
+        def give(b, inner):
+            sums = [
+                jnp.dot(
+                    pairs[parity],
+                    tab[:, pl.ds(pl.multiple_of(parity * span + b * half, half), half)],
+                    preferred_element_type=F32,
+                )
+                for parity in range(2)
+            ]
+            sums = jnp.concatenate(sums, axis=1)
+            deg = b * degrees + within_deg
+            split = (order_size, tile, degrees)
+            grad, curl = sums[:rows], sums[rows:]
+
+            def packed(inside, sign):
+                g = jnp.where(inside, sign * grad, 0.0).reshape(split)
+                c = jnp.where(inside, sign * curl, 0.0).reshape(split)
+                return jnp.concatenate([g, c], axis=1).astype(BF)
+
+            out2[s, :, b] = packed(deg >= m, 1.0)
+            out2[s, :, b + low] = packed(deg + low * degrees >= m, -1.0)
+            return inner
+
+        lax.fori_loop(0, low, give, 0)
+        land2[s, order_pos, blk] = out2[s, order_pos, blk]
+        send_all(second, s)
+        return carry
+
+    lax.fori_loop(0, group, process, 0)
+
+    for s in range(group):
+        await_all(second, s)
+        got = land2[s].astype(F32).reshape(devices, 2 * tile, degrees)
+        for k, ref in enumerate((grad_ref, curl_ref)):
+            z = got[:, k * tile : (k + 1) * tile].reshape(devices * tile, degrees).astype(BF)
+            value = turned(((0,), (0,)), z, pick[s])
+            if s:
+                value = value + ref[...].astype(F32)
+            ref[...] = value.astype(BF)
+
+    for s in range(group):
+        sent_all(first, s)
+        sent_all(second, s)
+
+
+def by_realization(order_size, blk_size, emode_coeffs, lensing_coeffs, order_values, circle_indices, circle_weights):
+    degrees, orders, csims = emode_coeffs.shape
+    lmax = degrees * blk_size
+    circle_total = circle_indices.shape[0]
+    devices = order_size * blk_size
+    group = csims // 2 // devices
+    width = orders * csims
+    tile = 2 * orders
+    rows = order_size * tile
+
+    def parted(coeffs):
+        return coeffs.reshape(degrees // 2, 2, width).transpose(1, 0, 2).reshape(degrees, width)
+
+    def joined(values):
+        return values.reshape(2, degrees // 2, orders, csims).transpose(1, 0, 2, 3).reshape(degrees, orders, csims)
+
+    dma = pltpu.SemaphoreType.DMA
+    mail = pltpu.VMEM((group, order_size, blk_size, 2 * tile, degrees), BF)
+    box = dma((group, order_size, blk_size))
+    grad, curl = pl.pallas_call(
+        functools.partial(
+            realization_kernel, lmax, circle_total, order_size, blk_size, orders, csims, group
+        ),
+        out_shape=[jax.ShapeDtypeStruct((degrees, width), BF)] * 2,
+        in_specs=[VMEM] * 5,
+        out_specs=[VMEM, VMEM],
+        scratch_shapes=[
+            pltpu.VMEM((group, devices * tile, width), BF),
+            mail, mail, mail, mail,
+            pltpu.VMEM((circle_total, lmax // 2), BF),
+            pltpu.VMEM((4 * rows, lmax // 2), BF),
+            pltpu.VMEM((6, rows, circle_total), BF),
+            pltpu.VMEM((2, 2, LONGS, rows), BF),
+            pltpu.VMEM((2, rows, LONGS), BF),
+            pltpu.VMEM((2, rows, circle_total), BF),
+            pltpu.VMEM((2, 2 * rows, circle_total), BF),
+            pltpu.VMEM((1, circle_total), F32),
+            box, box, box, box,
+        ],
+        compiler_params=pltpu.CompilerParams(
+            vmem_limit_bytes=48 << 20, collective_id=2, has_side_effects=True
+        ),
+        name="remap",
+    )(
+        parted(emode_coeffs),
+        parted(lensing_coeffs),
+        order_values.reshape(1, -1),
+        circle_indices.reshape(-1, 128),
+        circle_weights.reshape(-1, 128),
+    )
+    return joined(grad), joined(curl)
+
+
+def splits_by_realization(order_size, blk_size, emode_coeffs, circle_indices):
+    degrees, orders, csims = emode_coeffs.shape
+    circle_total = circle_indices.shape[0]
+    return (
+        (csims // 2) % (order_size * blk_size) == 0
+        and orders == 4
+        and blk_size % 2 == 0
+        and degrees % 256 == 0
+        and degrees * blk_size == 4 * circle_total
+        and circle_total % 512 == 0
+    )
+
+
+def body(order_size, blk_size, *arrays):
+    if splits_by_realization(order_size, blk_size, arrays[0], arrays[3]):
+        return by_realization(order_size, blk_size, *arrays)
+    return by_circle(order_size, blk_size, *arrays)
+
+
 def solution(mesh):
     in_specs = (P("blk", "order", None), P("blk", "order", None), P(), P(), P())
     out_specs = (P("blk", "order", None), P("blk", "order", None))

time: 109 us -> 66.7 us (0.61)
  Pallas kernels: 101 us -> 60.4 us
  local copies, waits for them, and re-layouts: 6.49 us -> 5.37 us
    pallas_call x3 -> x1, Pallas kernels: 101 us -> 60.4 us  [by_realization(): pl.pallas_call(functools.partial(realization_kernel, lmax, circle_total,...]
where the time goes in v1:
time: 66.7 us; the launch traced here: 66.5 us
  Pallas kernels  60.4 us (91%)
  local copies, waits for them, and re-layouts  5.37 us (8%)
  between operations  0.71 us (1%)
    pallas_call x1, Pallas kernels, by_realization(): pl.pallas_call(functools.partial(realization_kernel, lmax, circle_total,...  60.4 us
    transpose x2, local copies, waits for them, and re-layouts, joined(): values.reshape(2, degrees // 2, orders, csims).transpose(1, 0, 2, 3)  1.95 us
    unnamed x8, local copies, waits for them, and re-layouts  1.63 us
    reshape x4, local copies, waits for them, and re-layouts, parted(): coeffs.reshape(degrees // 2, 2, width).transpose(1, 0, 2)  1.55 us

profile of v1, /device:TPU:0, one launch (start us, length us, event | category | flops | bytes accessed | tf_op | source)
XLA Modules:
  0.0 66.5 jit_solution(6815180261687898001)
XLA Ops:
  0.6 1.2 %reshape.37 = bf16[256,2,512]{2,1,0:T(2,128)(2,1)S(1)} reshape(bf16[512,4,128]{2,1,0:T(4,128)(2,1)} %param.5) | data formatting | bytes 1048576 | tf_op jit(solution)/shard_map/reshape | solution.py:942
  1.9 0.0 copy-start.3
  1.9 0.1 copy.7
  1.9 1.0 %copy-done.3 = bf16[512,4,128]{2,1,0:T(4,128)(2,1)S(1)} copy-done((bf16[512,4,128]{2,1,0:T(4,128)(2,1)S(1)}, bf16[512,4,128]{2,1,0:T(4,128)(2,1)}, u32[]{:S(2)}) %copy-start.3) | copy-done | bytes 524312
  2.9 0.2 reshape.39
  3.1 0.0 copy-start
  3.1 0.0 copy-start.1
  3.1 0.1 copy.8
  3.2 0.0 copy-start.2
  3.2 0.6 copy-done
  3.8 0.0 copy-done.1
  3.8 0.0 copy-done.2
  3.9 60.4 %remap.1 = (bf16[512,512]{1,0:T(8,128)(2,1)S(1)}, bf16[512,512]{1,0:T(8,128)(2,1)S(1)}) custom-call(bf16[512,512]{1,0:T(8,128)(2,1)S(1)} %bitcast.13, bf16[512,512]{1,0:T(8,128)(2,1)S(1)} %bitcast.14, s32[1,16]{1,0:T(1,128)S(1)} %bitcast.17, s32[8,128]{1,0:T(8,128)S(1)} %bitcast.15, f32[8,128]{1,0:T(8,128)S(1)} %bitcast.16), custom_call_target="tpu_custom_call" | custom-call | tf_op jit(solution)/shard_map/remap/pallas_call | solution.py:950
  64.3 0.1 reshape.44
  64.4 1.0 %copy.9 = bf16[256,2,4,128]{3,2,1,0:T(4,128)(2,1)} copy(bf16[256,2,4,128]{3,2,0,1:T(4,128)(2,1)S(1)} %bitcast.18) | data formatting | bytes 1048576 | tf_op jit(solution)/shard_map/transpose | solution.py:945
  65.4 0.1 reshape.46
  65.5 1.0 %copy.10 = bf16[256,2,4,128]{3,2,1,0:T(4,128)(2,1)} copy(bf16[256,2,4,128]{3,2,0,1:T(4,128)(2,1)S(1)} %bitcast.19) | data formatting | bytes 1048576 | tf_op jit(solution)/shard_map/transpose | solution.py:945
Async XLA Ops:
  1.9 1.0 %copy-start.3 = (bf16[512,4,128]{2,1,0:T(4,128)(2,1)S(1)}, bf16[512,4,128]{2,1,0:T(4,128)(2,1)}, u32[]{:S(2)}) copy-start(bf16[512,4,128]{2,1,0:T(4,128)(2,1)} %param.6) | copy-start | bytes 1572868
  3.1 0.7 %copy-start = (s32[1024]{0:T(1024)S(1)}, s32[1024]{0:T(1024)}, u32[]{:S(2)}) copy-start(s32[1024]{0:T(1024)} %param.8) | copy-start | bytes 12292
  3.1 0.7 %copy-start.1 = (f32[1024]{0:T(1024)S(1)}, f32[1024]{0:T(1024)}, u32[]{:S(2)}) copy-start(f32[1024]{0:T(1024)} %param.9) | copy-start | bytes 12292
  3.2 0.7 copy-start.2

commit v2 on v1

--- a/solution.py
+++ b/solution.py
@@ -667,21 +667,32 @@
     full = 8 * circle_total
     width = orders * csims
 
-    def peer(k):
-        to_order = lax.rem(order_pos + (order_size - 1) - lax.rem(k, order_size), order_size)
-        to_blk = lax.rem(blk + (blk_size - 1) - lax.div(k, order_size), blk_size)
-        return to_order, to_blk
-
-    def hand(src, dst, send, recv, s, k):
-        o, b = peer(k)
+    late_from = blk_size - blk_size // 4
+    early = blk < late_from
+    early_total = order_size * late_from
+    late_total = devices - early_total
+
+    def each(begin, end, act):
+        def one(k, carry):
+            b = begin + lax.div(k, order_size)
+            o = lax.rem(order_pos + lax.rem(k, order_size), order_size)
+
+            @pl.when((o != order_pos) | (b != blk))
+            def _():
+                act(o, b)
+
+            return carry
+
+        lax.fori_loop(0, (end - begin) * order_size, one, 0)
+
+    def hand(src, dst, send, recv, s, o, b):
         return pltpu.make_async_remote_copy(
             src_ref=src.at[s, o, b], dst_ref=dst.at[s, order_pos, blk],
             send_sem=send.at[s, o, b], recv_sem=recv.at[s, order_pos, blk],
             device_id={"order": o, "blk": b}, device_id_type=MESH,
         )
 
-    def arrival(src, dst, send, recv, s, k):
-        o, b = peer(k)
+    def arrival(src, dst, send, recv, s, o, b):
         return pltpu.make_async_remote_copy(
             src_ref=src.at[s, o, b], dst_ref=dst.at[s, o, b],
             send_sem=send.at[s, o, b], recv_sem=recv.at[s, o, b],
@@ -691,35 +702,35 @@
     first = (out1, land1, s1, r1)
     second = (out2, land2, s2, r2)
 
+    def send_to(args, s, begin, end):
+        each(begin, end, lambda o, b: hand(*args, s, o, b).start())
+
     def send_all(args, s):
-        def one(k, carry):
-            hand(*args, s, k).start()
-            return carry
-
-        lax.fori_loop(0, devices - 1, one, 0)
+        each(0, blk_size, lambda o, b: hand(*args, s, o, b).start())
 
     def await_all(args, s):
-        def one(k, carry):
-            arrival(*args, s, k).wait_recv()
-            return carry
-
-        lax.fori_loop(0, devices - 1, one, 0)
+        each(0, blk_size, lambda o, b: arrival(*args, s, o, b).wait_recv())
 
     def sent_all(args, s):
-        def one(k, carry):
-            hand(*args, s, k).wait_send()
-            return carry
-
-        lax.fori_loop(0, devices - 1, one, 0)
+        each(0, blk_size, lambda o, b: hand(*args, s, o, b).wait_send())
 
     barrier = pltpu.get_barrier_semaphore()
 
-    def greet_one(k, carry):
-        o, b = peer(k)
-        pl.semaphore_signal(barrier, inc=1, device_id={"order": o, "blk": b}, device_id_type=MESH)
-        return carry
-
-    lax.fori_loop(0, devices - 1, greet_one, 0)
+    def hail(begin, end):
+        each(
+            begin, end,
+            lambda o, b: pl.semaphore_signal(
+                barrier, inc=1, device_id={"order": o, "blk": b}, device_id_type=MESH
+            ),
+        )
+
+    @pl.when(early)
+    def _():
+        hail(0, late_from)
+
+    @pl.when(jnp.logical_not(early))
+    def _():
+        hail(late_from, blk_size)
 
     def arrange(s):
         row = lax.broadcasted_iota(jnp.int32, (devices * tile, 1), 0)
@@ -737,10 +748,29 @@
         out1[s] = both.reshape(order_size, blk_size, 2 * tile, degrees)
         land1[s, order_pos, blk] = out1[s, order_pos, blk]
 
-    for s in range(group):
+    arrange(0)
+
+    @pl.when(early)
+    def _():
+        pl.semaphore_wait(barrier, early_total - 1)
+        hail(late_from, blk_size)
+        send_to(first, 0, 0, late_from)
+
+    @pl.when(jnp.logical_not(early))
+    def _():
+        pl.semaphore_wait(barrier, devices - 1)
+        hail(0, late_from)
+        send_to(first, 0, 0, blk_size)
+
+    for s in range(1, group):
         arrange(s)
-        if s == 0:
-            pl.semaphore_wait(barrier, devices - 1)
+
+    @pl.when(early)
+    def _():
+        pl.semaphore_wait(barrier, late_total)
+        send_to(first, 0, late_from, blk_size)
+
+    for s in range(1, group):
         send_all(first, s)
 
     amplitude = math.sqrt(2.0 / lmax)

time: 66.7 us -> 61.8 us (0.927)
  the two profiles are of different devices: /device:TPU:0 before, /device:TPU:21 now
where the time goes in v2:
time: 61.8 us; the launch traced here: 61.5 us
  Pallas kernels  55.5 us (90%)
  local copies, waits for them, and re-layouts  5.37 us (9%)
  between operations  0.71 us (1%)
    pallas_call x1, Pallas kernels, by_realization(): pl.pallas_call(functools.partial(realization_kernel, lmax, circle_total,...  55.5 us
    transpose x2, local copies, waits for them, and re-layouts, joined(): values.reshape(2, degrees // 2, orders, csims).transpose(1, 0, 2, 3)  1.95 us
    unnamed x8, local copies, waits for them, and re-layouts  1.63 us
    reshape x4, local copies, waits for them, and re-layouts, parted(): coeffs.reshape(degrees // 2, 2, width).transpose(1, 0, 2)  1.55 us

profile of v2, /device:TPU:21, one launch (start us, length us, event | category | flops | bytes accessed | tf_op | source)
XLA Modules:
  0.0 61.5 jit_solution(3368547128456613875)
XLA Ops:
  0.6 1.2 %reshape.37 = bf16[256,2,512]{2,1,0:T(2,128)(2,1)S(1)} reshape(bf16[512,4,128]{2,1,0:T(4,128)(2,1)} %param.5) | data formatting | bytes 1048576 | tf_op jit(solution)/shard_map/reshape | solution.py:972
  1.9 0.0 copy-start.3
  1.9 0.1 copy.7
  1.9 1.0 %copy-done.3 = bf16[512,4,128]{2,1,0:T(4,128)(2,1)S(1)} copy-done((bf16[512,4,128]{2,1,0:T(4,128)(2,1)S(1)}, bf16[512,4,128]{2,1,0:T(4,128)(2,1)}, u32[]{:S(2)}) %copy-start.3) | copy-done | bytes 524312
  2.9 0.2 reshape.39
  3.1 0.0 copy-start
  3.1 0.0 copy-start.1
  3.1 0.1 copy.8
  3.2 0.0 copy-start.2
  3.2 0.6 copy-done
  3.8 0.0 copy-done.1
  3.8 0.0 copy-done.2
  3.9 55.5 %remap.1 = (bf16[512,512]{1,0:T(8,128)(2,1)S(1)}, bf16[512,512]{1,0:T(8,128)(2,1)S(1)}) custom-call(bf16[512,512]{1,0:T(8,128)(2,1)S(1)} %bitcast.13, bf16[512,512]{1,0:T(8,128)(2,1)S(1)} %bitcast.14, s32[1,16]{1,0:T(1,128)S(1)} %bitcast.17, s32[8,128]{1,0:T(8,128)S(1)} %bitcast.15, f32[8,128]{1,0:T(8,128)S(1)} %bitcast.16), custom_call_target="tpu_custom_call" | custom-call | tf_op jit(solution)/shard_map/remap/pallas_call | solution.py:980
  59.3 0.1 reshape.44
  59.5 1.0 %copy.9 = bf16[256,2,4,128]{3,2,1,0:T(4,128)(2,1)} copy(bf16[256,2,4,128]{3,2,0,1:T(4,128)(2,1)S(1)} %bitcast.18) | data formatting | bytes 1048576 | tf_op jit(solution)/shard_map/transpose | solution.py:975
  60.4 0.1 reshape.46
  60.6 1.0 %copy.10 = bf16[256,2,4,128]{3,2,1,0:T(4,128)(2,1)} copy(bf16[256,2,4,128]{3,2,0,1:T(4,128)(2,1)S(1)} %bitcast.19) | data formatting | bytes 1048576 | tf_op jit(solution)/shard_map/transpose | solution.py:975
Async XLA Ops:
  1.9 1.0 %copy-start.3 = (bf16[512,4,128]{2,1,0:T(4,128)(2,1)S(1)}, bf16[512,4,128]{2,1,0:T(4,128)(2,1)}, u32[]{:S(2)}) copy-start(bf16[512,4,128]{2,1,0:T(4,128)(2,1)} %param.6) | copy-start | bytes 1572868
  3.1 0.7 %copy-start = (s32[1024]{0:T(1024)S(1)}, s32[1024]{0:T(1024)}, u32[]{:S(2)}) copy-start(s32[1024]{0:T(1024)} %param.8) | copy-start | bytes 12292
  3.1 0.7 %copy-start.1 = (f32[1024]{0:T(1024)S(1)}, f32[1024]{0:T(1024)}, u32[]{:S(2)}) copy-start(f32[1024]{0:T(1024)} %param.9) | copy-start | bytes 12292
  3.2 0.7 %copy-start.2 = (s32[16]{0:T(128)S(1)}, s32[16]{0:T(128)}, u32[]{:S(2)}) copy-start(s32[16]{0:T(128)} %param.7) | copy-start | bytes 196

commit v3 on v2

--- a/solution.py
+++ b/solution.py
@@ -648,14 +648,15 @@
 
 def realization_kernel(
     lmax, circle_total, order_size, blk_size, orders, csims, group,
-    em_ref, le_ref, m_ref, ci_ref, cw_ref, grad_ref, curl_ref,
+    em_ref, le_ref, m_any, ci_any, cw_any, grad_ref, curl_ref,
+    raw, wide, flat_in, m_ref, ci_ref, cw_ref,
     pick, out1, land1, out2, land2, tab, xs, maps, waves, waves_t, ana, pairs, wlane,
-    s1, r1, s2, r2,
+    s1, r1, s2, r2, pull,
 ):
     order_pos, blk = lax.axis_index("order"), lax.axis_index("blk")
     devices = order_size * blk_size
     me = order_pos * blk_size + blk
-    degrees = em_ref.shape[0]
+    degrees = em_ref.shape[0] // orders
     half = degrees // 2
     sims = csims // 2
     low = blk_size // 2
@@ -667,6 +668,15 @@
     full = 8 * circle_total
     width = orders * csims
 
+    pulls = [
+        pltpu.make_async_copy(src, dst, pull.at[k])
+        for k, (src, dst) in enumerate(
+            ((em_ref, raw.at[0]), (le_ref, raw.at[1]), (m_any, m_ref), (ci_any, ci_ref), (cw_any, cw_ref))
+        )
+    ]
+    for copy in pulls:
+        copy.start()
+
     late_from = blk_size - blk_size // 4
     early = blk < late_from
     early_total = order_size * late_from
@@ -732,7 +742,21 @@
     def _():
         hail(late_from, blk_size)
 
-    def arrange(s):
+    def strands():
+        for o in range(orders):
+            for parity in range(2):
+                yield (
+                    pl.ds(o + orders * parity, half, stride=2 * orders),
+                    slice(parity * half, (parity + 1) * half), slice(o * csims, (o + 1) * csims),
+                )
+
+    def unpack(k):
+        pulls[k].wait()
+        wide[k] = raw[k].astype(F32)
+        for mixed, rows_at, lanes_at in strands():
+            flat_in[k, rows_at, lanes_at] = wide[k, mixed, :].astype(BF)
+
+    def choose(s):
         row = lax.broadcasted_iota(jnp.int32, (devices * tile, 1), 0)
         within = lax.rem(row, tile)
         column = (
@@ -741,13 +765,18 @@
         lane = lax.broadcasted_iota(jnp.int32, (devices * tile, width), 1)
         choice = jnp.where(lane == column, 1.0, 0.0).astype(BF)
         pick[s] = choice
+
+    def arrange(s):
         split = (devices, tile, degrees)
-        e = turned(((1,), (1,)), choice, em_ref[...]).reshape(split)
-        p = turned(((1,), (1,)), choice, le_ref[...]).reshape(split)
+        e = turned(((1,), (1,)), pick[s], flat_in[0]).reshape(split)
+        p = turned(((1,), (1,)), pick[s], flat_in[1]).reshape(split)
         both = jnp.concatenate([e, p], axis=1).astype(BF)
         out1[s] = both.reshape(order_size, blk_size, 2 * tile, degrees)
         land1[s, order_pos, blk] = out1[s, order_pos, blk]
 
+    choose(0)
+    for k in range(2):
+        unpack(k)
     arrange(0)
 
     @pl.when(early)
@@ -763,6 +792,7 @@
         send_to(first, 0, 0, blk_size)
 
     for s in range(1, group):
+        choose(s)
         arrange(s)
 
     @pl.when(early)
@@ -773,6 +803,8 @@
     for s in range(1, group):
         send_all(first, s)
 
+    for copy in pulls[2:]:
+        copy.wait()
     amplitude = math.sqrt(2.0 / lmax)
     chunk = 64
 
@@ -949,9 +981,13 @@
         for k, ref in enumerate((grad_ref, curl_ref)):
             z = got[:, k * tile : (k + 1) * tile].reshape(devices * tile, degrees).astype(BF)
             value = turned(((0,), (0,)), z, pick[s])
-            if s:
-                value = value + ref[...].astype(F32)
-            ref[...] = value.astype(BF)
+            for mixed, rows_at, lanes_at in strands():
+                part = value[rows_at, lanes_at]
+                if s:
+                    part = part + wide[k, mixed, :]
+                wide[k, mixed, :] = part
+            if s == group - 1:
+                ref[...] = wide[k].astype(BF)
 
     for s in range(group):
         sent_all(first, s)
@@ -968,12 +1004,6 @@
     tile = 2 * orders
     rows = order_size * tile
 
-    def parted(coeffs):
-        return coeffs.reshape(degrees // 2, 2, width).transpose(1, 0, 2).reshape(degrees, width)
-
-    def joined(values):
-        return values.reshape(2, degrees // 2, orders, csims).transpose(1, 0, 2, 3).reshape(degrees, orders, csims)
-
     dma = pltpu.SemaphoreType.DMA
     mail = pltpu.VMEM((group, order_size, blk_size, 2 * tile, degrees), BF)
     box = dma((group, order_size, blk_size))
@@ -981,10 +1011,16 @@
         functools.partial(
             realization_kernel, lmax, circle_total, order_size, blk_size, orders, csims, group
         ),
-        out_shape=[jax.ShapeDtypeStruct((degrees, width), BF)] * 2,
-        in_specs=[VMEM] * 5,
+        out_shape=[jax.ShapeDtypeStruct((degrees * orders, csims), BF)] * 2,
+        in_specs=[pl.BlockSpec(memory_space=pl.ANY)] * 5,
         out_specs=[VMEM, VMEM],
         scratch_shapes=[
+            pltpu.VMEM((2, degrees * orders, csims), BF),
+            pltpu.VMEM((2, degrees * orders, csims), F32),
+            pltpu.VMEM((2, degrees, width), BF),
+            pltpu.VMEM((1, order_values.shape[0]), jnp.int32),
+            pltpu.VMEM((circle_total // 128, 128), jnp.int32),
+            pltpu.VMEM((circle_total // 128, 128), F32),
             pltpu.VMEM((group, devices * tile, width), BF),
             mail, mail, mail, mail,
             pltpu.VMEM((circle_total, lmax // 2), BF),
@@ -996,19 +1032,20 @@
             pltpu.VMEM((2, 2 * rows, circle_total), BF),
             pltpu.VMEM((1, circle_total), F32),
             box, box, box, box,
+            dma((5,)),
         ],
         compiler_params=pltpu.CompilerParams(
-            vmem_limit_bytes=48 << 20, collective_id=2, has_side_effects=True
+            vmem_limit_bytes=55200000, collective_id=2, has_side_effects=True
         ),
         name="remap",
     )(
-        parted(emode_coeffs),
-        parted(lensing_coeffs),
+        emode_coeffs.reshape(degrees * orders, csims),
+        lensing_coeffs.reshape(degrees * orders, csims),
         order_values.reshape(1, -1),
         circle_indices.reshape(-1, 128),
         circle_weights.reshape(-1, 128),
     )
-    return joined(grad), joined(curl)
+    return grad.reshape(emode_coeffs.shape), curl.reshape(emode_coeffs.shape)
 
 
 def splits_by_realization(order_size, blk_size, emode_coeffs, circle_indices):

time: 61.8 us -> 59.1 us (0.956)
  local copies, waits for them, and re-layouts: 5.37 us -> 2.27 us
    transpose x2 -> x0, local copies, waits for them, and re-layouts: 1.95 us -> none  [joined(): values.reshape(2, degrees // 2, orders, csims).transpose(1, 0, 2, 3)]
    reshape x6 -> x0, local copies, waits for them, and re-layouts: 1.79 us -> none  [the longest x4 1.55 us: parted(): coeffs.reshape(degrees // 2, 2, width).transpose(1, 0, 2)]
    unnamed x8, local copies, waits for them, and re-layouts: 1.63 us -> 2.27 us
where the time goes in v3:
time: 59.1 us; the launch traced here: 58.9 us
  Pallas kernels  56 us (95%)
  local copies, waits for them, and re-layouts  2.27 us (4%)
  between operations  0.66 us (1%)
    pallas_call x1, Pallas kernels, by_realization(): pl.pallas_call(functools.partial(realization_kernel, lmax, circle_total,...  56 us
    unnamed x8, local copies, waits for them, and re-layouts  2.27 us

profile of v3, /device:TPU:21, one launch (start us, length us, event | category | flops | bytes accessed | tf_op | source)
XLA Modules:
  0.0 58.9 jit_solution(3540076143590370728)
XLA Ops:
  0.6 0.0 copy-start.1
  0.6 0.0 copy-start
  0.7 0.0 copy-start.2
  0.7 0.7 %copy-done.1 = f32[1024]{0:T(1024)S(1)} copy-done((f32[1024]{0:T(1024)S(1)}, f32[1024]{0:T(1024)}, u32[]{:S(2)}) %copy-start.1) | copy-done | bytes 4120
  1.3 0.0 copy-done
  1.3 0.0 copy-done.2
  1.3 56.0 %remap.1 = (bf16[2048,128]{1,0:T(8,128)(2,1)S(1)}, bf16[2048,128]{1,0:T(8,128)(2,1)S(1)}) custom-call(bf16[2048,128]{1,0:T(8,128)(2,1)} %bitcast.12, bf16[2048,128]{1,0:T(8,128)(2,1)} %bitcast.13, s32[1,16]{1,0:T(1,128)S(1)} %bitcast.11, s32[8,128]{1,0:T(8,128)S(1)} %bitcast.9, f32[8,128]{1,0:T(8,128)S(1)} %bitcast.10), custom_call_target="tpu_custom_call" | custom-call | tf_op jit(solution)/shard_map/remap/pallas_call | solution.py:1010
  57.3 0.8 %copy.9 = bf16[512,4,128]{2,1,0:T(4,128)(2,1)} copy(bf16[512,4,128]{2,1,0:T(4,128)(2,1)S(1)} %bitcast.8) | data formatting | bytes 1048576
  58.1 0.8 %copy.10 = bf16[512,4,128]{2,1,0:T(4,128)(2,1)} copy(bf16[512,4,128]{2,1,0:T(4,128)(2,1)S(1)} %bitcast.7) | data formatting | bytes 1048576
Async XLA Ops:
  0.6 0.7 %copy-start.1 = (f32[1024]{0:T(1024)S(1)}, f32[1024]{0:T(1024)}, u32[]{:S(2)}) copy-start(f32[1024]{0:T(1024)} %param.9) | copy-start | bytes 12292
  0.6 0.7 %copy-start = (s32[1024]{0:T(1024)S(1)}, s32[1024]{0:T(1024)}, u32[]{:S(2)}) copy-start(s32[1024]{0:T(1024)} %param.8) | copy-start | bytes 12292
  0.7 0.7 %copy-start.2 = (s32[16]{0:T(128)S(1)}, s32[16]{0:T(128)}, u32[]{:S(2)}) copy-start(s32[16]{0:T(128)} %param.7) | copy-start | bytes 196

commit v4 on v3

--- a/solution.py
+++ b/solution.py
@@ -529,6 +529,7 @@
 
 SMEM = pl.BlockSpec(memory_space=pltpu.SMEM)
 VMEM = pl.BlockSpec(memory_space=pltpu.VMEM)
+HBM = pl.BlockSpec(memory_space=pltpu.HBM)
 PARAMS = pltpu.CompilerParams(vmem_limit_bytes=48 << 20)
 
 
@@ -994,6 +995,17 @@
         sent_all(second, s)
 
 
+def store_kernel(grad_ref, curl_ref, grad_out, curl_out, done):
+    copies = [
+        pltpu.make_async_copy(src, dst, done.at[k])
+        for k, (src, dst) in enumerate(((grad_ref, grad_out), (curl_ref, curl_out)))
+    ]
+    for copy in copies:
+        copy.start()
+    for copy in copies:
+        copy.wait()
+
+
 def by_realization(order_size, blk_size, emode_coeffs, lensing_coeffs, order_values, circle_indices, circle_weights):
     degrees, orders, csims = emode_coeffs.shape
     lmax = degrees * blk_size
@@ -1045,6 +1057,15 @@
         circle_indices.reshape(-1, 128),
         circle_weights.reshape(-1, 128),
     )
+    grad, curl = pl.pallas_call(
+        store_kernel,
+        out_shape=[jax.ShapeDtypeStruct(grad.shape, BF)] * 2,
+        in_specs=[VMEM, VMEM],
+        out_specs=[HBM, HBM],
+        scratch_shapes=[dma((2,))],
+        compiler_params=pltpu.CompilerParams(vmem_limit_bytes=1 << 20),
+        name="store",
+    )(grad, curl)
     return grad.reshape(emode_coeffs.shape), curl.reshape(emode_coeffs.shape)
 
 

time: 59.1 us -> 58.5 us (0.990)
  local copies, waits for them, and re-layouts: 2.27 us -> 0.68 us
  Pallas kernels: 56 us -> 57 us
    unnamed x8 -> x6, local copies, waits for them, and re-layouts: 2.27 us -> 0.68 us
    pallas_call x0 -> x1, Pallas kernels: none -> 0.99 us  [by_realization(): pl.pallas_call(store_kernel, out_shape=[jax.ShapeDtypeStruct(grad.shape,...]
where the time goes in v4:
time: 58.5 us; the launch traced here: 58.3 us
  Pallas kernels  57 us (97%)
  local copies, waits for them, and re-layouts  0.68 us (1%)
  between operations  0.66 us (1%)
    pallas_call x1, Pallas kernels, by_realization(): pl.pallas_call(functools.partial(realization_kernel, lmax, circle_total,...  56 us

profile of v4, /device:TPU:21, one launch (start us, length us, event | category | flops | bytes accessed | tf_op | source)
XLA Modules:
  0.0 58.3 jit_solution(10871588155491009412)
XLA Ops:
  0.6 0.0 copy-start.1
  0.6 0.0 copy-start
  0.7 0.0 copy-start.2
  0.7 0.7 %copy-done.1 = f32[1024]{0:T(1024)S(1)} copy-done((f32[1024]{0:T(1024)S(1)}, f32[1024]{0:T(1024)}, u32[]{:S(2)}) %copy-start.1) | copy-done | bytes 4120
  1.3 0.0 copy-done
  1.3 0.0 copy-done.2
  1.3 56.0 %remap.1 = (bf16[2048,128]{1,0:T(8,128)(2,1)S(1)}, bf16[2048,128]{1,0:T(8,128)(2,1)S(1)}) custom-call(bf16[2048,128]{1,0:T(8,128)(2,1)} %bitcast.10, bf16[2048,128]{1,0:T(8,128)(2,1)} %bitcast.11, s32[1,16]{1,0:T(1,128)S(1)} %bitcast.9, s32[8,128]{1,0:T(8,128)S(1)} %bitcast.7, f32[8,128]{1,0:T(8,128)S(1)} %bitcast.8), custom_call_target="tpu_custom_call" | custom-call | tf_op jit(solution)/shard_map/remap/pallas_call | solution.py:1022
  57.3 1.0 %store.1 = (bf16[2048,128]{1,0:T(8,128)(2,1)}, bf16[2048,128]{1,0:T(8,128)(2,1)}) custom-call(bf16[2048,128]{1,0:T(8,128)(2,1)S(1)} %get-tuple-element.6.grad_ref, bf16[2048,128]{1,0:T(8,128)(2,1)S(1)} %get-tuple-element.7.curl_ref), custom_call_target="tpu_custom_call" | custom-call | tf_op jit(solution)/shard_map/store/pallas_call | solution.py:1060
Async XLA Ops:
  0.6 0.7 %copy-start.1 = (f32[1024]{0:T(1024)S(1)}, f32[1024]{0:T(1024)}, u32[]{:S(2)}) copy-start(f32[1024]{0:T(1024)} %param.9) | copy-start | bytes 12292
  0.6 0.7 %copy-start = (s32[1024]{0:T(1024)S(1)}, s32[1024]{0:T(1024)}, u32[]{:S(2)}) copy-start(s32[1024]{0:T(1024)} %param.8) | copy-start | bytes 12292
  0.7 0.7 %copy-start.2 = (s32[16]{0:T(128)S(1)}, s32[16]{0:T(128)}, u32[]{:S(2)}) copy-start(s32[16]{0:T(128)} %param.7) | copy-start | bytes 196
